TPU v7x, 32 devices: a whole 2x2x4 slice. The times are simulated.
32 devices in a mesh: dp: 32 (over z, y, x, core).
Axes of the slice: x: 2, y: 2, z: 4, core: 2. Of those that a mesh axis runs over, the one named last changes fastest.
Arguments:
- tokens: bfloat16 [8192, 960], P('dp'), may hold values from -6 to 6
- out_grad: bfloat16 [8192, 960], P('dp'), may hold values from -6 to 6
- segment_ids: int32 [32, 256], P('dp'), may hold values from 0 to 255, as said below
- positions: int32 [32, 256], P('dp'), may hold values from 0 to 255, as said below
- attn_weight: bfloat16 [960, 2560], P(None, 'dp'), as said below
- gate_weight: bfloat16 [960, 2560], P(None, 'dp'), may hold values from -0.1875 to 0.1875
- up_weight: bfloat16 [960, 2560], P(None, 'dp'), may hold values from -0.1875 to 0.1875
- down_weight: bfloat16 [2560, 960], P('dp'), may hold values from -0.15625 to 0.15625
- norm_gains: bfloat16 [1920], P('dp'), may hold values from 0.25 to 1.75
Outputs:
- block_out: bfloat16 [8192, 960], P('dp')
- tokens_grad: float32 [8192, 960], P('dp')
- attn_weight_grad: float32 [960, 2560], P(None, 'dp')
- gate_weight_grad: float32 [960, 2560], P(None, 'dp')
- up_weight_grad: float32 [960, 2560], P(None, 'dp')
- down_weight_grad: float32 [2560, 960], P('dp')
- norm_gains_grad: float32 [1920], P('dp')
Inputs may be any that keep to these rules, and one draw needn't show every extreme that they name: `segment_ids`: in every sequence the ids start at 0 and rise by one where a new document begins; some sequence has a new document at every token. `positions`: A token's offset from the first token of its document; some sequence is a single document. `attn_weight`: projection weights scaled by their fan-in.
All inputs are finite; a program needn't handle non-finite values.
Results may differ from a plain program's by a relative error of at most 0.01.
The roundings to bfloat16 on the way count: a program that leaves them out, or rounds other values in their place, can miss the bound.
Values may be sent and summed in bfloat16 or wider, within the bound.
A program may use at most 256 MiB of HBM per device.

v0:
```python
import jax
import jax.numpy as jnp
from jax import lax
from jax.sharding import PartitionSpec as P

HEADS = 15
KV_HEADS = 5
HEAD_DIM = 64
GROUP = 3
QD = 960
KD = 320
epsilon = 1e-05
rope_base = 10000.0
masked_score = -1e30


def product(form, left, right):
    return jnp.einsum(form, left, right, preferred_element_type=jnp.float32)


def contract(left, right, left_axis, right_axis):
    return lax.dot_general(
        left, right, (((left_axis,), (right_axis,)), ((), ())), preferred_element_type=jnp.float32
    )


def rotate_half(values):
    half_dim = values.shape[-1] // 2
    return jnp.concatenate([-values[..., half_dim:], values[..., :half_dim]], axis=-1)


def rope_tables(positions):
    half_dim = HEAD_DIM // 2
    inverse = rope_base ** (-2.0 * jnp.arange(half_dim).astype(jnp.float32) / HEAD_DIM)
    angles = positions.astype(jnp.float32)[:, None] * inverse[None, :]
    angles = jnp.concatenate([angles, angles], axis=-1)
    return (jnp.cos(angles)[:, None, :], jnp.sin(angles)[:, None, :])


def norm_rows(values, gain):
    inv_rms = lax.rsqrt(jnp.mean(values * values, axis=-1, keepdims=True) + epsilon)
    normed = values * inv_rms
    return (normed, inv_rms, (normed * gain.astype(jnp.float32)).astype(jnp.bfloat16))


def norm_back(grad_in, normed, inv_rms, gain):
    grad_normed = grad_in * gain.astype(jnp.float32)
    grad_gain = jnp.sum(grad_in * normed, axis=0)
    inner_mean = jnp.mean(grad_normed * normed, axis=-1, keepdims=True)
    return (inv_rms * (grad_normed - normed * inner_mean), grad_gain)


def allowed_pairs(segments):
    row_index = jnp.arange(segments.shape[0])
    same_doc = segments[:, None] == segments[None, :]
    return same_doc & (row_index[:, None] >= row_index[None, :])


def scores_of(queries, key_rows, allowed):
    scores = product("qhgd,shd->hgqs", queries, key_rows) * HEAD_DIM ** (-0.5)
    return jnp.where(allowed[None, None], scores, masked_score)


def attend(queries, key_rows, value_rows, allowed):
    scores = scores_of(queries, key_rows, allowed)
    row_max = jnp.max(scores, axis=-1, keepdims=True)
    weights = jnp.exp(scores - row_max)
    totals = jnp.sum(weights, axis=-1, keepdims=True)
    weights_low = (weights / totals).astype(jnp.bfloat16)
    mixed_heads = product("hgqs,shd->qhgd", weights_low, value_rows).astype(jnp.bfloat16)
    return (mixed_heads, row_max + jnp.log(totals))


def attend_back(queries, key_rows, value_rows, allowed, mixed_heads, log_totals, grad_heads):
    scores = scores_of(queries, key_rows, allowed)
    probs_back = jnp.exp(scores - log_totals)
    grad_values = product("hgqs,qhgd->shd", probs_back.astype(jnp.bfloat16), grad_heads)
    grad_probs = product("qhgd,shd->hgqs", grad_heads, value_rows)
    row_dot = jnp.sum(grad_heads.astype(jnp.float32) * mixed_heads.astype(jnp.float32), axis=-1)
    row_dot = jnp.transpose(row_dot, (1, 2, 0))[..., None]
    grad_scores = (probs_back * (grad_probs - row_dot) * HEAD_DIM ** (-0.5)).astype(jnp.bfloat16)
    grad_queries = product("hgqs,shd->qhgd", grad_scores, key_rows)
    grad_keys = product("hgqs,qhgd->shd", grad_scores, queries)
    return (grad_queries, grad_keys, grad_values)


def layer_forward(
    tokens, segments, positions, attn_weight, gate_weight, up_weight, down_weight, norm_gains
):
    seq_len = tokens.shape[0]
    model_width = tokens.shape[1]
    residual = tokens.astype(jnp.float32)
    normed_one, inv_one, input_one = norm_rows(residual, norm_gains[:model_width])
    projected = contract(input_one, attn_weight[:, : QD + 2 * KD], 1, 0)
    cosine, sine_tab = rope_tables(positions)
    query_part = projected[:, :QD].reshape(seq_len, HEADS, HEAD_DIM)
    key_part = projected[:, QD : QD + KD].reshape(seq_len, KV_HEADS, HEAD_DIM)
    queries = (query_part * cosine + rotate_half(query_part) * sine_tab).astype(jnp.bfloat16)
    queries = queries.reshape(seq_len, KV_HEADS, GROUP, HEAD_DIM)
    key_rows = (key_part * cosine + rotate_half(key_part) * sine_tab).astype(jnp.bfloat16)
    value_rows = projected[:, QD + KD :].reshape(seq_len, KV_HEADS, HEAD_DIM).astype(jnp.bfloat16)
    allowed = allowed_pairs(segments)
    mixed_heads, log_totals = attend(queries, key_rows, value_rows, allowed)
    mixed_flat = mixed_heads.reshape(seq_len, QD)
    middle = residual + contract(mixed_flat, attn_weight[:, QD + 2 * KD :], 1, 1)
    normed_two, inv_two, input_two = norm_rows(middle, norm_gains[model_width:])
    gate_act = contract(input_two, gate_weight, 1, 0)
    up_proj = contract(input_two, up_weight, 1, 0)
    hidden = (jax.nn.silu(gate_act) * up_proj).astype(jnp.bfloat16)
    output = middle + contract(hidden, down_weight, 1, 0)
    kept_state = {
        "normed_one": normed_one,
        "inv_one": inv_one,
        "input_one": input_one,
        "cosine": cosine,
        "sine_tab": sine_tab,
        "queries": queries,
        "key_rows": key_rows,
        "value_rows": value_rows,
        "allowed": allowed,
        "mixed_heads": mixed_heads,
        "log_totals": log_totals,
        "normed_two": normed_two,
        "inv_two": inv_two,
        "input_two": input_two,
        "gate_act": gate_act,
        "up_proj": up_proj,
        "hidden": hidden,
    }
    return (output.astype(jnp.bfloat16), kept_state)


def ffn_backward(out_grad, kept_state, gate_weight, up_weight, down_weight, norm_gains):
    model_width = out_grad.shape[1]
    gate_act = kept_state["gate_act"]
    input_two = kept_state["input_two"]
    grad_hidden = contract(out_grad, down_weight, 1, 1)
    grad_down = contract(kept_state["hidden"], out_grad, 0, 0)
    sig_gate = jax.nn.sigmoid(gate_act)
    grad_gate = (
        grad_hidden * kept_state["up_proj"] * sig_gate * (1.0 + gate_act * (1.0 - sig_gate))
    ).astype(jnp.bfloat16)
    grad_up = (grad_hidden * gate_act * sig_gate).astype(jnp.bfloat16)
    grad_gate_w = contract(input_two, grad_gate, 0, 0)
    grad_up_w = contract(input_two, grad_up, 0, 0)
    grad_input_two = contract(grad_gate, gate_weight, 1, 1) + contract(grad_up, up_weight, 1, 1)
    grad_norm_two, grad_gain_two = norm_back(
        grad_input_two, kept_state["normed_two"], kept_state["inv_two"], norm_gains[model_width:]
    )
    grad_middle = out_grad.astype(jnp.float32) + grad_norm_two
    return (grad_middle, grad_gain_two, (grad_gate_w, grad_up_w, grad_down))


def attn_backward(grad_middle, kept_state, attn_weight, norm_gains):
    seq_len = grad_middle.shape[0]
    model_width = grad_middle.shape[1]
    mixed_heads = kept_state["mixed_heads"]
    grad_mid_low = grad_middle.astype(jnp.bfloat16)
    grad_out_proj = contract(grad_mid_low, mixed_heads.reshape(seq_len, QD), 0, 0)
    grad_heads = contract(grad_mid_low, attn_weight[:, QD + 2 * KD :], 1, 0).astype(jnp.bfloat16)
    grad_heads = grad_heads.reshape(seq_len, KV_HEADS, GROUP, HEAD_DIM)
    grad_queries, grad_keys, grad_values = attend_back(
        kept_state["queries"],
        kept_state["key_rows"],
        kept_state["value_rows"],
        kept_state["allowed"],
        mixed_heads,
        kept_state["log_totals"],
        grad_heads,
    )
    cosine = kept_state["cosine"]
    sine_tab = kept_state["sine_tab"]
    grad_q_part = grad_queries.reshape(seq_len, HEADS, HEAD_DIM)
    grad_q_part = grad_q_part * cosine - rotate_half(grad_q_part) * sine_tab
    grad_k_part = grad_keys * cosine - rotate_half(grad_keys) * sine_tab
    grad_projected = jnp.concatenate(
        [
            grad_q_part.reshape(seq_len, QD),
            grad_k_part.reshape(seq_len, KD),
            grad_values.reshape(seq_len, KD),
        ],
        axis=1,
    ).astype(jnp.bfloat16)
    grad_qkv = contract(kept_state["input_one"], grad_projected, 0, 0)
    grad_input_one = contract(grad_projected, attn_weight[:, : QD + 2 * KD], 1, 1)
    grad_norm_one, grad_gain_one = norm_back(
        grad_input_one, kept_state["normed_one"], kept_state["inv_one"], norm_gains[:model_width]
    )
    grad_tokens = grad_middle + grad_norm_one
    grad_attn = jnp.concatenate([grad_qkv, grad_out_proj], axis=1)
    return (grad_tokens, grad_attn, grad_gain_one)


def device_rows(parts, devices):
    widths = [matrix.shape[dim] // devices for matrix, dim in parts]
    per_device = sum(widths)

    def term_rows(start, count):
        blocks_here = count // per_device
        blocks = []
        for (matrix, dim), width in zip(parts, widths):
            piece = matrix
            if dim == 1:
                piece = piece.T
            blocks.append(piece.reshape(blocks_here, width, piece.shape[1]))
        return jnp.concatenate(blocks, axis=1).reshape(blocks_here * per_device, -1)

    return (term_rows, widths, per_device)


def split_rows(summed, parts, widths):
    results = []
    offset = 0
    for (matrix, dim), width in zip(parts, widths):
        block = summed[offset : offset + width]
        results.append(block.T if dim == 1 else block)
        offset = offset + width
    return results


def on_device(
    tokens,
    out_grad,
    segment_ids,
    positions,
    attn_weight,
    gate_weight,
    up_weight,
    down_weight,
    norm_gains,
):
    devices = lax.axis_size("dp")
    gathered = (
        lax.all_gather(attn_weight, "dp", axis=1, tiled=True),
        lax.all_gather(gate_weight, "dp", axis=1, tiled=True),
        lax.all_gather(up_weight, "dp", axis=1, tiled=True),
        lax.all_gather(down_weight, "dp", axis=0, tiled=True),
        lax.all_gather(norm_gains, "dp", axis=0, tiled=True),
    )
    output, kept_state = layer_forward(
        tokens,
        segment_ids[0],
        positions[0],
        gathered[0],
        gathered[1],
        gathered[2],
        gathered[3],
        gathered[4],
    )
    grad_middle, grad_gain_two, ffn_grads = ffn_backward(
        out_grad, kept_state, gathered[1], gathered[2], gathered[3], gathered[4]
    )
    grad_tokens, grad_attn, grad_gain_one = attn_backward(
        grad_middle, kept_state, gathered[0], gathered[4]
    )
    grad_gains = jnp.concatenate([grad_gain_one, grad_gain_two])
    all_parts = [(grad_attn, 1), (ffn_grads[0], 1), (ffn_grads[1], 1), (ffn_grads[2], 0)]
    all_fn, all_widths, all_rows = device_rows(all_parts, devices)
    all_summed = lax.psum_scatter(
        all_fn(jnp.int32(0), all_rows * lax.axis_size("dp")), "dp", scatter_dimension=0, tiled=True
    )
    shares = tuple(split_rows(all_summed, all_parts, all_widths))
    gain_share = lax.psum_scatter(grad_gains, "dp", scatter_dimension=0, tiled=True)
    return (output, grad_tokens, shares[0], shares[1], shares[2], shares[3], gain_share)


def solution(mesh):
    in_specs = (
        P("dp", None),
        P("dp", None),
        P("dp", None),
        P("dp", None),
        P(None, "dp"),
        P(None, "dp"),
        P(None, "dp"),
        P("dp", None),
        P("dp"),
    )
    out_specs = (
        P("dp", None),
        P("dp", None),
        P(None, "dp"),
        P(None, "dp"),
        P(None, "dp"),
        P("dp", None),
        P("dp"),
    )
    return jax.shard_map(
        on_device, mesh=mesh, in_specs=in_specs, out_specs=out_specs, check_vma=False
    )
```

profile of v0, /device:TPU:1, one launch (start us, length us, event | category | flops | bytes accessed | tf_op | source)
XLA Modules:
  0.0 832.3 jit_solution(10276416389014661938)
XLA Ops:
  11.5 41.5 %all-reduce = bf16[1920]{0:T(1024)(128)(2,1)S(1)} all-reduce(bf16[1920]{0:T(1024)(128)(2,1)S(1)} %dynamic-update-slice), channel_id=1, replica_groups=mesh['dp'=32] {'dp'}, use_global_device_ids=true, to_apply=%add | all-reduce | flops 1920 | bytes 7680
  55.4 23.2 %all-gather.5.cloned.1.call-done = bf16[960,2560]{0,1:T(8,128)(2,1)} async-done(((bf16[960,80]{0,1:T(8,128)(2,1)}), bf16[960,2560]{0,1:T(8,128)(2,1)}) %all-gather.5.cloned.1.call-update) | async-done | bytes 4915216 | tf_op jit(solution)/shard_map/all_gather | solution.py:234
  78.7 3.1 fusion.7
  85.1 2.6 multiply_reduce_fusion.3
  88.0 57.3 %all-gather.9.cloned.1.call-done = bf16[960,2560]{0,1:T(8,128)(2,1)} async-done(((bf16[960,80]{0,1:T(8,128)(2,1)}), bf16[960,2560]{0,1:T(8,128)(2,1)}) %all-gather.9.cloned.1.call-update) | async-done | bytes 4915216 | tf_op jit(solution)/shard_map/all_gather | solution.py:236
  145.3 5.6 fusion.64
  150.9 61.1 %all-gather.7.cloned.1.call-done = bf16[960,2560]{0,1:T(8,128)(2,1)} async-done(((bf16[960,80]{0,1:T(8,128)(2,1)}), bf16[960,2560]{0,1:T(8,128)(2,1)}) %all-gather.7.cloned.1.call-update) | async-done | bytes 4915216 | tf_op jit(solution)/shard_map/all_gather | solution.py:235
  212.0 5.5 fusion.63
  217.6 61.0 %all-gather.11.cloned.1.call-done = bf16[2560,960]{1,0:T(8,128)(2,1)} async-done(((bf16[80,960]{1,0:T(8,128)(2,1)}), bf16[2560,960]{1,0:T(8,128)(2,1)}) %all-gather.11.cloned.1.call-update) | async-done | bytes 4915216 | tf_op jit(solution)/shard_map/all_gather | solution.py:237
  278.6 8.7 %multiply_convert_fusion = (bf16[256,2560]{1,0:T(8,128)(2,1)S(1)}, bf16[256,2560]{1,0:T(8,128)(2,1)S(1)}, bf16[256,2560]{1,0:T(8,128)(2,1)}) fusion(f32[256,2560]{1,0:T(8,128)} %fusion.63, f32[256,2560]{1,0:T(8,128)} %fusion.64, bf16[256,960]{0,1:T(8,128)(2,1)S(1)} %copy-done.3, bf16[2560,960]{1,0:T(8,128)(2,1)} %all-gather.11.cloned.1.call-done), kind=kOutput, calls=%fused_computation.16 | convolution fusion | flops 1268776960 | bytes 14581760 | tf_op jit(solution)/shard_map/dot_general | solution.py:22
  289.4 4.9 multiply_reduce_fusion
  300.4 2.6 fusion.51
  303.0 5.5 fusion.68
  308.5 5.4 fusion.67
  315.1 4.0 fusion.45
  319.1 9.6 %maximum_bitcast_fusion = f32[2560,960]{0,1:T(8,128)} fusion(f32[960,960]{1,0:T(8,128)} %fusion.51, f32[960,1600]{1,0:T(8,128)} %fusion.45), kind=kLoop, calls=%fused_computation.1 | loop fusion | flops 2457600 | bytes 19660800 | tf_op jit(solution)/shard_map/transpose | solution.py:204
  328.6 11.3 %copy.33 = f32[2560,960]{1,0:T(8,128)} copy(f32[2560,960]{0,1:T(8,128)} %maximum_bitcast_fusion) | data formatting | bytes 19660800 | tf_op jit(solution)/shard_map/transpose | solution.py:204
  339.9 6.8 fusion.69
  346.8 28.4 %pad_maximum_fusion = f32[32,320,960]{2,1,0:T(8,128)} fusion(f32[32,80,960]{2,1,0:T(8,128)} %bitcast.106, f32[32,80,960]{2,1,0:T(8,128)} %bitcast.104, f32[32,80,960]{2,1,0:T(8,128)} %bitcast.105, f32[32,80,960]{2,1,0:T(8,128)} %bitcast.107), kind=kLoop, calls=%fused_computation | loop fusion | flops 29491200 | bytes 78643200 | tf_op jit(solution)/shard_map/concatenate | solution.py:206
  376.2 4.4 fusion.39
  380.7 61.1 %all-reduce.1 = f32[1920]{0:T(1024)S(1)} all-reduce(f32[1920]{0:T(1024)S(1)} %pad_maximum_fusion.5), channel_id=3, replica_groups=mesh['dp'=32] {'dp'}, use_global_device_ids=true, to_apply=%region_10.11.clone | all-reduce | flops 1920 | bytes 15360
  442.4 2.4 fusion.38
  444.8 5.9 fusion.23
  450.7 372.7 %reduce-scatter.2.cloned.1.call-done = f32[320,960]{1,0:T(8,128)} async-done(((f32[10240,960]{1,0:T(8,128)}), f32[320,960]{1,0:T(8,128)}) %reduce-scatter.2.cloned.1.call-update) | async-done | bytes 1228816 | tf_op jit(solution)/shard_map/reduce_scatter | solution.py:259
  (89 shorter events, 23.3 us)
Async XLA Ops:
  7.2 71.5 %all-gather.5.cloned.1.call-start = ((), (), s32[]{:S(2)}) async-start(), calls=%async_computation.1 | async-start | bytes 5406720 | tf_op jit(solution)/shard_map/all_gather | solution.py:234
  7.9 137.4 %all-gather.9.cloned.1.call-start = ((), (), s32[]{:S(2)}) async-start(), calls=%async_computation.3 | async-start | bytes 5406720 | tf_op jit(solution)/shard_map/all_gather | solution.py:236
  8.6 203.4 %all-gather.7.cloned.1.call-start = ((), (), s32[]{:S(2)}) async-start(), calls=%async_computation.2 | async-start | bytes 5406720 | tf_op jit(solution)/shard_map/all_gather | solution.py:235
  9.4 269.2 %all-gather.11.cloned.1.call-start = ((), (), s32[]{:S(2)}) async-start(), calls=%async_computation.4 | async-start | bytes 5406720 | tf_op jit(solution)/shard_map/all_gather | solution.py:237
  10.0 813.5 %reduce-scatter.2.cloned.1.call-start = ((), (), s32[]{:S(2)}) async-start(), calls=%async_computation.5 | async-start | bytes 43253760 | tf_op jit(solution)/shard_map/reduce_scatter | solution.py:259
  53.3 28.9 %copy-start.8 = (f32[256,64]{0,1:T(8,128)}, f32[256,64]{0,1:T(8,128)S(1)}, u32[]{:S(2)}) copy-start(f32[256,64]{0,1:T(8,128)S(1)} %get-tuple-element.27) | copy-start | bytes 196612
  81.8 1.9 copy-start.12
  82.0 1.1 copy-start.10
  83.1 2.0 copy-start
  83.7 1.4 copy-start.2
  85.1 2.7 copy-start.6
  150.9 127.7 %copy-start.3 = (bf16[256,960]{0,1:T(8,128)(2,1)S(1)}, bf16[256,960]{0,1:T(8,128)(2,1)}, u32[]{:S(2)}) copy-start(bf16[256,960]{0,1:T(8,128)(2,1)} %param.10) | copy-start | bytes 1474564
  278.6 8.7 %copy-start.18 = (bf16[960,2560]{0,1:T(8,128)(2,1)S(1)}, bf16[960,2560]{0,1:T(8,128)(2,1)}, u32[]{:S(2)}) copy-start(bf16[960,2560]{0,1:T(8,128)(2,1)} %all-gather.7.cloned.1.call-done) | copy-start | bytes 14745604
  289.4 4.9 copy-start.4
  294.3 2.8 copy-start.7
  294.4 2.9 copy-start.1
  294.7 3.4 copy-start.13
  298.0 16.4 %copy-start.16 = (bf16[5,64,256]{2,1,0:T(8,128)(2,1)}, bf16[5,64,256]{2,1,0:T(8,128)(2,1)S(1)}, u32[]{:S(2)}) copy-start(bf16[5,64,256]{2,1,0:T(8,128)(2,1)S(1)} %fusion.31) | copy-start | bytes 491524
  298.1 1.9 copy-start.11
  308.5 5.5 copy-start.9
  314.4 0.7 copy-start.14
  328.6 11.3 %copy-start.5 = (bf16[256,960]{0,1:T(8,128)(2,1)S(1)}, bf16[256,960]{0,1:T(8,128)(2,1)}, u32[]{:S(2)}) copy-start(bf16[256,960]{0,1:T(8,128)(2,1)} %param.10) | copy-start | bytes 1474564
  375.2 0.9 copy-start.15
  375.2 1.0 copy-start.17
Sparse Core Ops, SparseCore 0:
  10.8 67.7 all-gather.4
  81.5 63.7 all-gather.8
  148.2 63.7 all-gather.6
  214.8 63.7 all-gather.10
  375.4 448.0 reduce-scatter.1
where the time goes:
time: 833 us; the launch traced here: 832 us
  waiting for transfers between devices  578 us (69%)
  blocking collectives  103 us (12%)
  matrix products  74.3 us (9%)
  other arithmetic  45.6 us (5%)
  local copies, waits for them, and re-layouts  17.4 us (2%)
  between operations  14.2 us (2%)
    reduce_scatter x1, waiting for transfers between devices, on_device(): lax.psum_scatter(all_fn(jnp.int32(0), all_rows * lax.axis_size('dp')), 'd...  373 us
    unnamed x2, blocking collectives  103 us
    dot_general x15, matrix products, contract(): lax.dot_general(left, right, (((left_axis,), (right_axis,)), ((), ())), p...  69.7 us
    all_gather x1, waiting for transfers between devices, on_device(): lax.all_gather(gate_weight, 'dp', axis=1, tiled=True)  61.1 us
    all_gather x1, waiting for transfers between devices, on_device(): lax.all_gather(down_weight, 'dp', axis=0, tiled=True)  61 us
    all_gather x1, waiting for transfers between devices, on_device(): lax.all_gather(up_weight, 'dp', axis=1, tiled=True)  57.3 us
    concatenate x1, other arithmetic, term_rows(): return jnp.concatenate(blocks, axis=1).reshape(blocks_here * per_device, -1)  28.4 us
    all_gather x1, waiting for transfers between devices, on_device(): lax.all_gather(attn_weight, 'dp', axis=1, tiled=True)  23.2 us
  transfers between devices with their start and end apart: 5, of which 5 were waited for; matrix products, arithmetic and copies ran while one was open for 4% of the time, Pallas kernels for 0%

commit v1 on v0

--- a/solution.py
+++ b/solution.py
@@ -12,6 +12,27 @@
 epsilon = 1e-05
 rope_base = 10000.0
 masked_score = -1e30
+
+
+def joined_along(blocks, dim):
+    blocks = jnp.moveaxis(blocks, 0, dim)
+    shape = blocks.shape
+    return blocks.reshape(*shape[:dim], shape[dim] * shape[dim + 1], *shape[dim + 2 :])
+
+
+def grow_blocks(x, axis):
+    size, place = (lax.axis_size(axis), lax.axis_index(axis))
+    pieces, stride = (x[None], 1)
+    while stride < size:
+        other = lax.ppermute(pieces, axis, [(i, i ^ stride) for i in range(size)])
+        low = place & stride == 0
+        pieces = jnp.concatenate([jnp.where(low, pieces, other), jnp.where(low, other, pieces)])
+        stride *= 2
+    return pieces
+
+
+def gather_by_bits(shard, axis, dim):
+    return joined_along(grow_blocks(shard, axis), dim)
 
 
 def product(form, left, right):
@@ -233,7 +254,7 @@
     gathered = (
         lax.all_gather(attn_weight, "dp", axis=1, tiled=True),
         lax.all_gather(gate_weight, "dp", axis=1, tiled=True),
-        lax.all_gather(up_weight, "dp", axis=1, tiled=True),
+        gather_by_bits(up_weight, "dp", 1),
         lax.all_gather(down_weight, "dp", axis=0, tiled=True),
         lax.all_gather(norm_gains, "dp", axis=0, tiled=True),
     )

time: 833 us -> 870 us (1.044)
  blocking collectives: 103 us -> 207 us
  waiting for transfers between devices: 578 us -> 500 us
    unnamed x2, blocking collectives: 103 us -> 207 us
    ppermute x0 -> x5, waiting for transfers between devices: none -> 73.4 us  [grow_blocks(): other = lax.ppermute(pieces, axis, [(i, i ^ stride) for i in range(size)])]
    all_gather x1, waiting for transfers between devices: 61 us -> 0.02 us  [on_device(): lax.all_gather(down_weight, 'dp', axis=0, tiled=True)]
    all_gather x1 -> x0, waiting for transfers between devices: 57.3 us -> none  [on_device(): lax.all_gather(up_weight, 'dp', axis=1, tiled=True)]
    all_gather x1, waiting for transfers between devices: 23.2 us -> 0.01 us  [on_device(): lax.all_gather(attn_weight, 'dp', axis=1, tiled=True)]
    all_gather x1, waiting for transfers between devices: 61.1 us -> 52.2 us  [on_device(): lax.all_gather(gate_weight, 'dp', axis=1, tiled=True)]
  transfers between devices with their start and end apart: 5 -> 9, of which waited for: 5 -> 6; matrix products, arithmetic and copies ran while one was open for 4% -> 4% of each run, Pallas kernels for 0% -> 0%
where the time goes in v1:
time: 870 us; the launch traced here: 869 us
  waiting for transfers between devices  500 us (57%)
  blocking collectives  207 us (24%)
  matrix products  69.9 us (8%)
  other arithmetic  53 us (6%)
  local copies, waits for them, and re-layouts  17.8 us (2%)
  between operations  14.2 us (2%)
    reduce_scatter x1, waiting for transfers between devices, on_device(): lax.psum_scatter(all_fn(jnp.int32(0), all_rows * lax.axis_size('dp')), 'd...  373 us
    unnamed x2, blocking collectives  207 us
    ppermute x5, waiting for transfers between devices, grow_blocks(): other = lax.ppermute(pieces, axis, [(i, i ^ stride) for i in range(size)])  73.4 us
    dot_general x15, matrix products, contract(): lax.dot_general(left, right, (((left_axis,), (right_axis,)), ((), ())), p...  65.2 us
    all_gather x1, waiting for transfers between devices, on_device(): lax.all_gather(gate_weight, 'dp', axis=1, tiled=True)  52.2 us
    concatenate x1, other arithmetic, term_rows(): return jnp.concatenate(blocks, axis=1).reshape(blocks_here * per_device, -1)  28.5 us
  transfers between devices with their start and end apart: 9, of which 6 were waited for; matrix products, arithmetic and copies ran while one was open for 4% of the time, Pallas kernels for 0%

profile of v1, /device:TPU:1, one launch (start us, length us, event | category | flops | bytes accessed | tf_op | source)
XLA Modules:
  0.0 868.8 jit_solution(16141494905438458641)
XLA Ops:
  13.8 7.7 collective-permute-done.1
  23.0 16.1 %collective-permute-done.2 = bf16[4,960,80]{1,2,0:T(8,128)(2,1)S(1)} collective-permute-done((bf16[4,960,80]{1,2,0:T(8,128)(2,1)S(1)}, bf16[4,960,80]{1,2,0:T(8,128)(2,1)S(1)}, u32[]{:S(2)}, u32[]{:S(2)}) %collective-permute-start.2) | collective-permute-done | bytes 614432 | tf_op jit(solution)/shard_map/ppermute | solution.py:27
  41.4 48.1 %collective-permute-done.3 = bf16[8,960,80]{1,2,0:T(8,128)(2,1)} collective-permute-done((bf16[8,960,80]{1,2,0:T(8,128)(2,1)S(1)}, bf16[8,960,80]{1,2,0:T(8,128)(2,1)}, u32[]{:S(2)}, u32[]{:S(2)}) %collective-permute-start.3) | collective-permute-done | bytes 1228832 | tf_op jit(solution)/shard_map/ppermute | solution.py:27
  94.5 146.0 %all-reduce = bf16[1920]{0:T(1024)(128)(2,1)S(1)} all-reduce(bf16[1920]{0:T(1024)(128)(2,1)S(1)} %dynamic-update-slice), channel_id=1, replica_groups=mesh['dp'=32] {'dp'}, use_global_device_ids=true, to_apply=%add | all-reduce | flops 1920 | bytes 7680
  243.3 2.9 pad_maximum_fusion.1
  246.2 3.1 fusion.7
  253.3 2.7 multiply_reduce_fusion.3
  256.3 5.6 fusion.64
  261.9 52.2 %all-gather.6.cloned.1.call-done = bf16[960,2560]{0,1:T(8,128)(2,1)} async-done(((bf16[960,80]{0,1:T(8,128)(2,1)}), bf16[960,2560]{0,1:T(8,128)(2,1)}) %all-gather.6.cloned.1.call-update) | async-done | bytes 4915216 | tf_op jit(solution)/shard_map/all_gather | solution.py:256
  314.2 4.2 fusion.63
  318.4 8.3 multiply_convert_fusion
  337.5 2.6 fusion.51
  340.1 5.6 fusion.68
  345.7 5.4 fusion.67
  351.5 4.0 fusion.45
  355.5 9.6 %maximum_bitcast_fusion = f32[2560,960]{0,1:T(8,128)} fusion(f32[960,960]{1,0:T(8,128)} %fusion.51, f32[960,1600]{1,0:T(8,128)} %fusion.45), kind=kLoop, calls=%fused_computation.1 | loop fusion | flops 2457600 | bytes 19660800 | tf_op jit(solution)/shard_map/transpose | solution.py:225
  365.1 11.2 %copy.33 = f32[2560,960]{1,0:T(8,128)} copy(f32[2560,960]{0,1:T(8,128)} %maximum_bitcast_fusion) | data formatting | bytes 19660800 | tf_op jit(solution)/shard_map/transpose | solution.py:225
  376.3 6.9 fusion.69
  383.2 28.5 %pad_maximum_fusion = f32[32,320,960]{2,1,0:T(8,128)} fusion(f32[32,80,960]{2,1,0:T(8,128)} %bitcast.112, f32[32,80,960]{2,1,0:T(8,128)} %bitcast.110, f32[32,80,960]{2,1,0:T(8,128)} %bitcast.111, f32[32,80,960]{2,1,0:T(8,128)} %bitcast.113), kind=kLoop, calls=%fused_computation | loop fusion | flops 29491200 | bytes 78643200 | tf_op jit(solution)/shard_map/concatenate | solution.py:227
  412.6 4.4 fusion.39
  417.1 61.3 %all-reduce.1 = f32[1920]{0:T(1024)S(1)} all-reduce(f32[1920]{0:T(1024)S(1)} %pad_maximum_fusion.10), channel_id=3, replica_groups=mesh['dp'=32] {'dp'}, use_global_device_ids=true, to_apply=%region_10.11.clone | all-reduce | flops 1920 | bytes 15360
  478.9 2.4 fusion.38
  481.4 5.5 fusion.23
  486.8 373.1 %reduce-scatter.2.cloned.1.call-done = f32[320,960]{1,0:T(8,128)} async-done(((f32[10240,960]{1,0:T(8,128)}), f32[320,960]{1,0:T(8,128)}) %reduce-scatter.2.cloned.1.call-update) | async-done | bytes 1228816 | tf_op jit(solution)/shard_map/reduce_scatter | solution.py:280
  (110 shorter events, 37.3 us)
Async XLA Ops:
  7.2 239.0 %all-gather.4.cloned.1.call-start = ((), (), s32[]{:S(2)}) async-start(), calls=%async_computation.1 | async-start | bytes 5406720 | tf_op jit(solution)/shard_map/all_gather | solution.py:255
  7.9 248.4 %all-gather.8.cloned.1.call-start = ((), (), s32[]{:S(2)}) async-start(), calls=%async_computation.3 | async-start | bytes 5406720 | tf_op jit(solution)/shard_map/all_gather | solution.py:258
  8.7 305.5 %all-gather.6.cloned.1.call-start = ((), (), s32[]{:S(2)}) async-start(), calls=%async_computation.2 | async-start | bytes 5406720 | tf_op jit(solution)/shard_map/all_gather | solution.py:256
  8.7 1.7 collective-permute-start
  11.4 10.1 %collective-permute-start.1 = (bf16[2,960,80]{1,2,0:T(8,128)(2,1)S(1)}, bf16[2,960,80]{1,2,0:T(8,128)(2,1)S(1)}, u32[]{:S(2)}, u32[]{:S(2)}) collective-permute-start(bf16[2,960,80]{1,2,0:T(8,128)(2,1)S(1)} %pad_maximum_fusion.8), channel_id=1, source_target_pairs={{0,2},{1,3},{2,0},{3,1},{4,6},{5,7},{6,4},{7,5},{8,10},{9,11},{10,... | collective-permute-start | bytes 921608 | tf_op jit(solution)/shard_map/ppermute | solution.py:27
  21.6 17.4 %collective-permute-start.2 = (bf16[4,960,80]{1,2,0:T(8,128)(2,1)S(1)}, bf16[4,960,80]{1,2,0:T(8,128)(2,1)S(1)}, u32[]{:S(2)}, u32[]{:S(2)}) collective-permute-start(bf16[4,960,80]{1,2,0:T(8,128)(2,1)S(1)} %pad_maximum_fusion.5), channel_id=1, source_target_pairs={{0,4},{1,5},{2,6},{3,7},{4,0},{5,1},{6,2},{7,3},{8,12},{9,13},{10,... | collective-permute-start | bytes 1843208 | tf_op jit(solution)/shard_map/ppermute | solution.py:27
  22.9 837.0 %reduce-scatter.2.cloned.1.call-start = ((), (), s32[]{:S(2)}) async-start(), calls=%async_computation.4 | async-start | bytes 43253760 | tf_op jit(solution)/shard_map/reduce_scatter | solution.py:280
  40.1 49.3 %collective-permute-start.3 = (bf16[8,960,80]{1,2,0:T(8,128)(2,1)S(1)}, bf16[8,960,80]{1,2,0:T(8,128)(2,1)}, u32[]{:S(2)}, u32[]{:S(2)}) collective-permute-start(bf16[8,960,80]{1,2,0:T(8,128)(2,1)S(1)} %pad_maximum_fusion.3), channel_id=1, source_target_pairs={{0,8},{1,9},{2,10},{3,11},{4,12},{5,13},{6,14},{7,15},{8,0},{9,1},... | collective-permute-start | bytes 3686408 | tf_op jit(solution)/shard_map/ppermute | solution.py:27
  91.1 3.1 copy-start.14
  91.1 3.1 copy-start.15
  91.1 149.6 %copy-start.3 = (bf16[256,960]{0,1:T(8,128)(2,1)S(1)}, bf16[256,960]{0,1:T(8,128)(2,1)}, u32[]{:S(2)}) copy-start(bf16[256,960]{0,1:T(8,128)(2,1)} %param.9) | copy-start | bytes 1474564
  91.2 149.8 %copy-start.13 = (s32[1,256]{1,0:T(1,128)S(1)}, s32[1,256]{1,0:T(1,128)}, u32[]{:S(2)}) copy-start(s32[1,256]{1,0:T(1,128)} %param.11) | copy-start | bytes 3076
  92.9 148.2 %collective-permute-start.4 = (bf16[16,960,80]{1,2,0:T(8,128)(2,1)}, bf16[16,960,80]{1,2,0:T(8,128)(2,1)}, u32[]{:S(2)}, u32[]{:S(2)}) collective-permute-start(bf16[16,960,80]{1,2,0:T(8,128)(2,1)} %pad_maximum_fusion.2), channel_id=1, source_target_pairs={{0,16},{1,17},{2,18},{3,19},{4,20},{5,21},{6,22},{7,23},{8,24},{9,... | collective-permute-start | bytes 7372808 | tf_op jit(solution)/shard_map/ppermute | solution.py:27
  253.3 2.9 copy-start.8
  253.3 3.0 copy-start.6
  314.2 12.6 %slice-start.2 = ((s8[5242880]{0:T(1024)(128)(4,1)}), s8[4194304]{0:T(1024)(128)(4,1)S(1)}, s32[]{:S(2)}) async-start(s8[5242880]{0:T(1024)(128)(4,1)} %bitcast.140), calls=%async_computation.7 | async-start | bytes 8388608
  314.2 14.8 %slice-start = ((s8[5242880]{0:T(1024)(128)(4,1)}), s8[4194304]{0:T(1024)(128)(4,1)S(1)}, s32[]{:S(2)}) async-start(s8[5242880]{0:T(1024)(128)(4,1)} %bitcast.115), calls=%async_computation.5 | async-start | bytes 8388608
  318.4 8.4 slice-start.3
  318.4 10.5 %slice-start.1 = ((s8[5242880]{0:T(1024)(128)(4,1)}), s8[1048576]{0:T(1024)(128)(4,1)S(1)}, s32[]{:S(2)}) async-start(s8[5242880]{0:T(1024)(128)(4,1)} %bitcast.115), calls=%async_computation.6 | async-start | bytes 2097152
  329.0 2.4 copy-start.7
  331.3 2.7 copy-start.9
  331.7 2.7 copy-start.1
  335.2 16.4 %copy-start.11 = (bf16[5,64,256]{2,1,0:T(8,128)(2,1)}, bf16[5,64,256]{2,1,0:T(8,128)(2,1)S(1)}, u32[]{:S(2)}) copy-start(bf16[5,64,256]{2,1,0:T(8,128)(2,1)S(1)} %fusion.31) | copy-start | bytes 491524
  478.3 3.0 copy-start.10
  (5 other events, 5.7 us)
Sparse Core Ops, SparseCore 0:
  10.8 77.3 all-gather.3
  91.1 155.9 all-gather.7
  250.0 64.1 all-gather.5
  411.8 448.0 reduce-scatter.1
